TPU v7x, 32 devices: a whole 2x2x4 slice. The times are simulated.
32 devices in a mesh: samp: 8 (over z, x), snp: 4 (over y, core).
Axes of the slice: x: 2, y: 2, z: 4, core: 2. Of those that a mesh axis runs over, the one named last changes fastest.
Arguments:
- genotype: bfloat16 [16384, 1024], P('samp', 'snp'), may hold values from -60 to 60
- phenotype: float32 [16384], P('samp'), may hold values from -6 to 6
- residual: float32 [16384], P('samp'), may hold values from -6 to 6
- sign_flips: int32 [16384, 127], P('samp'), may hold values from -1 to 1, as said below
- weights: bfloat16 [128, 49, 128], P('snp'), may hold values from -0.5 to 0.5
- member: int32 [128, 49], P('snp'), may hold values 0 or 1
- gene_start: int32 [128], P('snp'), may hold values from 0 to 1023, as said below
- gene_end: int32 [128], P('snp'), may hold values from 1 to 1024, as said below
Outputs:
- z_scores: float32 [128, 49, 128], P('snp')
Inputs may be any that keep to these rules, and one draw needn't show every extreme that they name: `sign_flips`: each entry is -1 or 1. `gene_start`: gene g's start lies among the SNPs of block g // 32 of 256 SNPs, at or past (g % 32) * (8) within it and before the next such mark, except that the last gene starts at 1023; the first gene starts at 0. gene_end - gene_start lies between 1 and 128 and reaches 128 in every block of genes except possibly the last; gene_end is at most 1024, and the last gene ends at 1024.
All inputs are finite; a program needn't handle non-finite values. No bound on the sum of `member` on one device may be relied on, other than what follows from the above.
Results may differ from a plain program's by a relative error of at most 0.0041.
Values may be sent and summed in bfloat16 or wider, within the bound.
A program may use at most 64 MiB of HBM per device.

v0:
```python
import jax
import jax.numpy as jnp
from jax import lax
from jax.sharding import PartitionSpec as P


def shifted(array, axis, by):
    count = lax.axis_size(axis)
    pairs = [(i, i + by) for i in range(count) if 0 <= i + by < count]
    return lax.ppermute(array, axis, pairs)


def finish(cross_prod, col_mean, col_spread, lab_part, scale_root):
    return (cross_prod - col_mean[:, None] * lab_part[None, :]) / (col_spread[:, None] * scale_root)


def on_device(genotype, phenotype, residual, sign_flips, weights, member, gene_start, gene_end):
    sample_local, snp_local = genotype.shape
    gene_local, tissue_count, window_len = weights.shape
    halo_cols = shifted(genotype[:, :window_len], "snp", -1)
    extended = jnp.concatenate([genotype, halo_cols], axis=1)
    offset = lax.axis_index("snp") * snp_local
    local_start = gene_start - offset
    window_pos = jnp.arange(window_len, dtype=jnp.int32)
    inside_mask = (window_pos[None, :] < (gene_end - gene_start)[:, None]).astype(jnp.float32)
    window_wts = (
        weights.astype(jnp.float32)
        * member.astype(jnp.float32)[:, :, None]
        * inside_mask[:, None, :]
    ).astype(jnp.bfloat16)
    column_pos = jnp.arange(snp_local + window_len, dtype=jnp.int32)
    one_hot = (
        column_pos[None, :, None] == local_start[:, None, None] + window_pos[None, None, :]
    ).astype(jnp.bfloat16)
    banded = jnp.einsum("gsj,gtj->sgt", one_hot, window_wts, preferred_element_type=jnp.float32)
    banded = banded.astype(jnp.bfloat16).reshape(snp_local + window_len, gene_local * tissue_count)
    predicted = jnp.dot(extended, banded, preferred_element_type=jnp.float32).astype(jnp.bfloat16)
    labels = jnp.concatenate(
        [phenotype[:, None], residual[:, None] * sign_flips.astype(jnp.float32)], axis=1
    ).astype(jnp.bfloat16)
    wide_pred = predicted.astype(jnp.float32)
    sum_pred = jnp.sum(wide_pred, axis=0)
    sum_sq = jnp.sum(wide_pred * wide_pred, axis=0)
    sum_lab = jnp.sum(labels.astype(jnp.float32), axis=0)
    cross_prod = jnp.einsum("nc,nk->ck", predicted, labels, preferred_element_type=jnp.float32)
    sample_total = sample_local * lax.axis_size("samp")
    scale_root = jnp.sqrt(jnp.asarray(sample_total, dtype=jnp.float32))
    cross_prod, sum_pred, sum_sq, sum_lab = lax.psum(
        (cross_prod, sum_pred, sum_sq, sum_lab), "samp"
    )
    col_mean = sum_pred / sample_total
    col_spread = jnp.sqrt(sum_sq / sample_total - col_mean * col_mean + 1e-06)
    z_scores = finish(cross_prod, col_mean, col_spread, sum_lab, scale_root)
    return z_scores.reshape(gene_local, tissue_count, z_scores.shape[1])


def solution(mesh):
    return jax.shard_map(
        on_device,
        mesh=mesh,
        in_specs=(
            P("samp", "snp"),
            P("samp"),
            P("samp"),
            P("samp", None),
            P("snp", None, None),
            P("snp", None),
            P("snp"),
            P("snp"),
        ),
        out_specs=P("snp", None, None),
        check_vma=False,
    )
```

profile of v0, /device:TPU:0, one launch (start us, length us, event | category | flops | bytes accessed | tf_op | source)
XLA Modules:
  0.0 113.8 jit_solution(10013964653927407819)
XLA Ops:
  6.5 0.0 all-reduce.3.cloned.1.call-start
  6.5 1.1 slice.3
  7.6 0.0 copy-start.1
  7.6 1.3 %collective-permute-start = (bf16[2048,128]{1,0:T(8,128)(2,1)S(1)}, bf16[2048,128]{1,0:T(8,128)(2,1)}, u32[]{:S(2)}, u32[]{:S(2)}) collective-permute-start(bf16[2048,128]{1,0:T(8,128)(2,1)S(1)} %slice.3), channel_id=1, source_target_pairs={{1,0},{2,1},{3,2},{5,4},{6,5},{7,6},{9,8},{10,9},{11,10},{13,12},{... | collective-permute-start | bytes 1572872 | tf_op jit(solution)/shard_map/ppermute | solution.py:10
  8.9 0.7 fusion.13
  9.6 0.1 iota_add_fusion
  9.7 0.1 fusion.10
  9.8 0.7 convert_element_type.37
  10.5 0.1 copy.12
  10.6 0.0 copy-start
  10.6 1.3 %multiply_convert_fusion.1 = bf16[32,49,128]{2,0,1:T(8,128)(2,1)S(1)} fusion(bf16[32,49,128]{2,0,1:T(8,128)(2,1)} %param.12, f32[32,128]{1,0:T(8,128)S(1)} %fusion.10, f32[32,49]{0,1:T(8,128)S(1)} %copy.12), kind=kLoop, calls=%fused_computation.15 | loop fusion | flops 802816 | bytes 825472 | tf_op jit(solution)/shard_map/convert_element_type | solution.py:30
  11.9 1.9 %fusion.7 = bf16[384,32,49]{0,2,1:T(8,128)(2,1)S(1)} fusion(s32[32,128]{1,0:T(8,128)S(1)} %iota_add_fusion, bf16[32,49,128]{2,0,1:T(8,128)(2,1)S(1)} %multiply_convert_fusion.1), kind=kOutput, calls=%fused_computation.11 | convolution fusion | flops 156315648 | bytes 1622016 | tf_op jit(solution)/shard_map/gsj,gtj->sgt/dot_general | solution.py:35
  13.7 0.4 reshape.51
  14.2 0.0 copy-done.1
  14.2 0.3 broadcast_in_dim.4
  14.5 0.0 copy-done
  14.6 1.6 %multiply_convert_fusion = bf16[2048,127]{1,0:T(8,128)(2,1)S(1)} fusion(s32[2048,127]{1,0:T(8,128)} %param.11, f32[2048]{0:T(1024)S(1)} %copy-done), kind=kLoop, calls=%fused_computation.13 | loop fusion | flops 780288 | bytes 1568768 | tf_op jit(solution)/shard_map/convert.1
  16.1 0.0 collective-permute-done
  16.1 5.2 %convert_reduce_fusion = (f32[1568]{0:T(1024)S(1)}, f32[1568]{0:T(1024)S(1)}, bf16[2048,1568]{0,1:T(8,128)(2,1)S(1)}) fusion(bf16[384,1568]{0,1:T(8,128)(2,1)S(1)} %reshape.51, bf16[2048,128]{1,0:T(8,128)(2,1)} %collective-permute-done, bf16[2048,256]{1,0:T(8,128)(2,1)} %param.8), kind=kOutput, calls=%fused_computation.1 | convolution fusion | flops 2485449728 | bytes 9212160 | tf_op jit(solution)/shard_map/dot_general | solution.py:37
  21.4 2.9 %fusion.9 = f32[1568,128]{1,0:T(8,128)} fusion(bf16[2048,1568]{0,1:T(8,128)(2,1)S(1)} %get-tuple-element.14, bf16[2048,127]{1,0:T(8,128)(2,1)S(1)} %multiply_convert_fusion, bf16[2048,1]{1,0:T(8,128)(2,1)S(1)} %broadcast_in_dim.4), kind=kOutput, calls=%fused_computation.18 | convolution fusion | flops 823132160 | bytes 7749632 | tf_op jit(solution)/shard_map/nc,nk->ck/dot_general | solution.py:45
  24.2 0.0 all-reduce.3.cloned.1.call-update
  24.3 0.4 convert_reduce_fusion.1
  24.6 39.0 %all-reduce = (f32[1568]{0:T(1024)S(1)}, f32[1568]{0:T(1024)S(1)}, f32[128]{0:T(128)S(1)}) all-reduce(f32[1568]{0:T(1024)S(1)} %get-tuple-element.6, f32[1568]{0:T(1024)S(1)} %get-tuple-element.5, f32[128]{0:T(128)S(1)} %convert_reduce_fusion.1), channel_id=1, replica_groups=mesh['samp'=8,'snp'=4] {'samp'}, use_global_device_ids=true, to_apply=%region_6.0 | all-reduce | flops 3264 | bytes 26112 | tf_op jit(solution)/shard_map/psum | solution.py:48
  63.7 40.6 %all-reduce.3.cloned.1.call-done = f32[1568,128]{1,0:T(8,128)} async-done(((f32[1568,128]{1,0:T(8,128)}), f32[1568,128]{1,0:T(8,128)}) %all-reduce.3.cloned.1.call-update) | async-done | bytes 802832 | tf_op jit(solution)/shard_map/psum | solution.py:48
  104.2 1.6 %subtract_divide_fusion = f32[1568,128]{1,0:T(8,128)S(1)} fusion(f32[1568,128]{1,0:T(8,128)} %all-reduce.3.cloned.1.call-done, f32[1568]{0:T(1024)S(1)} %get-tuple-element.11, f32[128]{0:T(128)S(1)} %get-tuple-element.9, f32[1568]{0:T(1024)S(1)} %get-tuple-element.10), kind=kLoop, calls=%fused_computation.14 | loop fusion | flops 602112 | bytes 1618688 | tf_op jit(solution)/shard_map/div | solution.py:14
  105.8 0.1 reshape.52
  105.9 1.0 copy.15
  (2 shorter events, 0.0 us)
Async XLA Ops:
  6.5 97.7 %all-reduce.3.cloned.1.call-start = ((), (), s32[]{:S(2)}) async-start(), calls=%async_computation | async-start | bytes 1605632 | tf_op jit(solution)/shard_map/psum | solution.py:48
  7.6 6.6 %copy-start.1 = (f32[2048]{0:T(1024)S(1)}, f32[2048]{0:T(1024)}, u32[]{:S(2)}) copy-start(f32[2048]{0:T(1024)} %param.9) | copy-start | bytes 24580
  7.6 8.5 %collective-permute-start = (bf16[2048,128]{1,0:T(8,128)(2,1)S(1)}, bf16[2048,128]{1,0:T(8,128)(2,1)}, u32[]{:S(2)}, u32[]{:S(2)}) collective-permute-start(bf16[2048,128]{1,0:T(8,128)(2,1)S(1)} %slice.3), channel_id=1, source_target_pairs={{1,0},{2,1},{3,2},{5,4},{6,5},{7,6},{9,8},{10,9},{11,10},{13,12},{... | collective-permute-start | bytes 1572872 | tf_op jit(solution)/shard_map/ppermute | solution.py:10
  10.6 4.0 %copy-start = (f32[2048]{0:T(1024)S(1)}, f32[2048]{0:T(1024)}, u32[]{:S(2)}) copy-start(f32[2048]{0:T(1024)} %param.10) | copy-start | bytes 24580
Sparse Core Ops, SparseCore 0:
  24.4 79.7 all-reduce.2
where the time goes:
time: 114 us
  waiting for transfers between devices  40.6 us (36%)
  blocking collectives  39 us (34%)
  between operations  13.5 us (12%)
  matrix products  9.96 us (9%)
  other arithmetic  6.38 us (6%)
  local copies, waits for them, and re-layouts  3.03 us (3%)
  starting transfers between devices  1.29 us (1%)
    psum x1, waiting for transfers between devices, on_device(): lax.psum((cross_prod, sum_pred, sum_sq, sum_lab), 'samp')  40.6 us
    psum x1, blocking collectives, on_device(): lax.psum((cross_prod, sum_pred, sum_sq, sum_lab), 'samp')  39 us
    dot_general x1, matrix products, on_device(): jnp.dot(extended, banded, preferred_element_type=jnp.float32)  5.24 us
    dot_general x1, matrix products, on_device(): jnp.einsum('nc,nk->ck', predicted, labels, preferred_element_type=jnp.flo...  2.85 us
  transfers between devices with their start and end apart: 2, of which 1 were waited for; matrix products, arithmetic and copies ran while one was open for 7% of the time, Pallas kernels for 0%

commit v1 on v0

v1 whole, which is shorter than its diff:
```python
import functools

import jax
import jax.numpy as jnp
from jax import lax
from jax.experimental import pallas as pl
from jax.experimental.pallas import tpu as pltpu
from jax.sharding import PartitionSpec as P

MESH = pl.DeviceIdType.MESH
TILE = 16
PARTS = 4


def across(left, right):
    return lax.dot_general(left, right, (((0,), (0,)), ((), ())), preferred_element_type=jnp.float32)


def iotas(rows, cols):
    return (
        lax.broadcasted_iota(jnp.int32, (rows, cols), 0),
        lax.broadcasted_iota(jnp.int32, (rows, cols), 1),
    )


def share_of(rows, count):
    per = -(-rows // (count * TILE)) * TILE
    while rows % per:
        per += TILE
    return per


def columns_of(rows_ref):
    tiles, width = rows_ref.shape
    block = rows_ref[...]
    if tiles < width:
        block = jnp.concatenate([block, jnp.zeros((width - tiles, width), jnp.float32)], axis=0)
    return block.T


def sums_kernel(
    count, ring, window,
    geno, phen, resid, flips,
    near_out, far_out, sums_out,
    geno_v, flips_v, halo_v, labels_v,
    early_s, early_r, early_p, early_g,
    late_s, late_r, late_p, late_g,
    tail_v, tail_sums, sums_s, sums_r, sums_t,
    load_sem, flip_sem, halo_ss, halo_rs,
    es_ss, es_rs, eg_ss, eg_rs, ls_ss, ls_rs, lg_ss, lg_rs,
    sm_ss, sm_rs, tl_ss, tl_rs,
):
    me = lax.axis_index("samp")
    mine = lax.axis_index("snp")
    before = lax.rem(mine + ring - 1, ring)
    after = lax.rem(mine + 1, ring)
    samples, snps = geno_v.shape
    blocks = snps // window
    part = samples // PARTS

    loads, flip_loads = [], []
    for i in range(PARTS):
        rows = pl.ds(i * part, part)
        loads.append(pltpu.make_async_copy(geno.at[rows], geno_v.at[rows], load_sem.at[i]))
        flip_loads.append(pltpu.make_async_copy(flips.at[rows], flips_v.at[rows], flip_sem.at[i]))
        loads[i].start()
        flip_loads[i].start()

    def peers(body):
        if count <= 16:
            for dist in range(1, count):
                body(dist)
        else:
            def step(dist, carry):
                body(dist)
                return carry
            lax.fori_loop(1, count, step, 0)

    def ahead(dist):
        return lax.rem(me + dist, count)

    def behind(dist):
        return lax.rem(me + count - dist, count)

    barrier = pltpu.get_barrier_semaphore()
    peers(lambda dist: pl.semaphore_signal(
        barrier, inc=1, device_id=(ahead(dist), mine), device_id_type=MESH))
    for other in (before, after):
        pl.semaphore_signal(barrier, inc=1, device_id=(me, other), device_id_type=MESH)
    pl.semaphore_wait(barrier, count + 1)

    def remote(src, dst, ss, rs, device):
        return pltpu.make_async_remote_copy(
            src_ref=src, dst_ref=dst, send_sem=ss, recv_sem=rs,
            device_id=device, device_id_type=MESH)

    halos = []
    for i in range(PARTS):
        rows = pl.ds(i * part, part)
        halos.append(remote(
            geno.at[rows, pl.ds(0, window)], halo_v.at[rows],
            halo_ss.at[i], halo_rs.at[i], (me, before)))
        halos[i].start()

    def guarded(owners, index, body):
        if owners == count:
            body()
        else:
            pl.when(index < owners)(body)

    def scatter_copy(buf, got, ss, rs, per, dist):
        start = pl.multiple_of(ahead(dist) * per, TILE)
        return remote(buf.at[pl.ds(start, per)], got.at[dist], ss.at[dist], rs.at[dist], (ahead(dist), mine))

    def gather_copy(piece, full, ss, rs, per, dist):
        start = pl.multiple_of(me * per, TILE)
        return remote(piece, full.at[pl.ds(start, per)], ss.at[dist], rs.at[dist], (ahead(dist), mine))

    def scatter_start(buf, got, ss, rs, per):
        owners = buf.shape[0] // per
        peers(lambda dist: guarded(
            owners, ahead(dist), lambda: scatter_copy(buf, got, ss, rs, per, dist).start()))

    def reduce_and_gather(buf, got, piece, full, ss, rs, gss, grs, per):
        owners = buf.shape[0] // per

        def owner():
            start = pl.multiple_of(me * per, TILE)
            rows = pl.ds(start, per)
            total = buf[rows, :].astype(jnp.float32)
            if count <= 16:
                for dist in range(1, count):
                    scatter_copy(buf, got, ss, rs, per, dist).wait_recv()
                    total += got[dist].astype(jnp.float32)
            else:
                def step(dist, total):
                    scatter_copy(buf, got, ss, rs, per, dist).wait_recv()
                    return total + got[dist].astype(jnp.float32)
                total = lax.fori_loop(1, count, step, total)
            piece[...] = total.astype(piece.dtype)
            peers(lambda dist: gather_copy(piece, full, gss, grs, per, dist).start())
            full[rows, :] = piece[...]
        guarded(owners, me, owner)

    def gather_wait(buf, piece, full, gss, grs, per):
        owners = buf.shape[0] // per

        def one(dist):
            start = pl.multiple_of(behind(dist) * per, TILE)
            guarded(owners, behind(dist), lambda: remote(
                piece, full.at[pl.ds(start, per)], gss.at[dist], grs.at[dist], (ahead(dist), mine)).wait_recv())
        peers(one)

    def sends_wait(buf, got, piece, full, ss, rs, gss, grs, per):
        owners = buf.shape[0] // per
        peers(lambda dist: guarded(
            owners, ahead(dist), lambda: scatter_copy(buf, got, ss, rs, per, dist).wait_send()))
        guarded(owners, me, lambda: peers(
            lambda dist: gather_copy(piece, full, gss, grs, per, dist).wait_send()))

    flip_count = flips_v.shape[1]
    phen_cols = columns_of(phen)
    resid_cols = columns_of(resid)
    lanes = phen.shape[1]
    for i in range(PARTS):
        flip_loads[i].wait()
        for t in range(i * part // lanes, (i + 1) * part // lanes):
            rows = pl.ds(t * lanes, lanes)
            signs = flips_v[rows, :].astype(jnp.float32)
            labels_v[rows, pl.ds(0, flip_count)] = (signs * resid_cols[:, t:t + 1]).astype(jnp.bfloat16)
            labels_v[rows, pl.ds(flip_count, 1)] = phen_cols[:, t:t + 1].astype(jnp.bfloat16)

    for i in range(PARTS):
        loads[i].wait()
    own = geno_v[...]
    labels = labels_v[...]
    with_labels = across(own, labels)
    gram = across(own, own)
    ones = jnp.ones((8, samples), jnp.bfloat16)
    col_sums = jnp.dot(ones, own, preferred_element_type=jnp.float32)
    lab_sums = jnp.dot(ones, labels, preferred_element_type=jnp.float32)
    row8, _ = iotas(8, window)
    sums = jnp.where(row8 == blocks, lab_sums, 0.0)
    for b in range(blocks):
        sums = jnp.where(row8 == b, col_sums[:, b * window:(b + 1) * window], sums)
    sums_s[...] = sums

    def sums_copy(dist):
        return remote(sums_s, sums_r.at[dist], sm_ss.at[dist], sm_rs.at[dist], (ahead(dist), mine))

    row, col = iotas(window, window)
    early_s[pl.ds(0, window), :] = with_labels[0:window].astype(jnp.bfloat16)
    for b in range(blocks - 1):
        low, mid, high = b * window, (b + 1) * window, (b + 2) * window
        band = jnp.where(col >= row, gram[low:mid, low:mid], gram[low:mid, mid:high])
        early_s[pl.ds((1 + b) * window, window), :] = band.astype(jnp.bfloat16)
        early_s[pl.ds((blocks + b) * window, window), :] = with_labels[mid:high].astype(jnp.bfloat16)
    early_per, late_per = early_p.shape[0], late_p.shape[0]
    scatter_start(early_s, early_r, es_ss, es_rs, early_per)
    peers(lambda dist: sums_copy(dist).start())

    last = snps - window
    with_halo = jnp.zeros((window, window), jnp.float32)
    for i in range(PARTS):
        rows = pl.ds(i * part, part)
        halos[i].wait_recv()
        with_halo += across(geno_v[rows, pl.ds(last, window)], halo_v[rows, :])
    late_s[...] = jnp.where(col >= row, gram[last:, last:], with_halo).astype(jnp.bfloat16)
    scatter_start(late_s, late_r, ls_ss, ls_rs, late_per)

    reduce_and_gather(early_s, early_r, early_p, early_g, es_ss, es_rs, eg_ss, eg_rs, early_per)

    sums_total = sums_s[...]
    if count <= 16:
        for dist in range(1, count):
            sums_copy(dist).wait_recv()
            sums_total += sums_r[dist]
    else:
        def step(dist, total):
            sums_copy(dist).wait_recv()
            return total + sums_r[dist]
        sums_total = lax.fori_loop(1, count, step, sums_total)
    sums_t[...] = sums_total
    tail_copies = [remote(sums_t, tail_sums, tl_ss.at[0], tl_rs.at[0], (me, before))]
    tail_copies[0].start()

    reduce_and_gather(late_s, late_r, late_p, late_g, ls_ss, ls_rs, lg_ss, lg_rs, late_per)

    gather_wait(early_s, early_p, early_g, eg_ss, eg_rs, early_per)
    tail_copies.append(remote(
        early_g.at[pl.ds(0, 2 * window)], tail_v, tl_ss.at[1], tl_rs.at[1], (me, before)))
    tail_copies[1].start()
    near_out[pl.ds(0, early_g.shape[0]), :] = early_g[...]
    gather_wait(late_s, late_p, late_g, lg_ss, lg_rs, late_per)
    near_out[pl.ds(early_g.shape[0], window), :] = late_g[...]
    sums_out[pl.ds(0, 8), :] = sums_t[...]
    for copy in tail_copies:
        copy.wait_recv()
    far_out[...] = tail_v[...]
    sums_out[pl.ds(8, 8), :] = tail_sums[...]

    for copy in halos + tail_copies:
        copy.wait_send()
    sends_wait(early_s, early_r, early_p, early_g, es_ss, es_rs, eg_ss, eg_rs, early_per)
    sends_wait(late_s, late_r, late_p, late_g, ls_ss, ls_rs, lg_ss, lg_rs, late_per)
    peers(lambda dist: sums_copy(dist).wait_send())


def reduced_sums(genotype, phenotype, residual, sign_flips, window):
    samples, snps = genotype.shape
    count, ring = lax.axis_size("samp"), lax.axis_size("snp")
    blocks = snps // window
    early_rows = (2 * blocks - 1) * window
    early_per, late_per = share_of(early_rows, count), share_of(window, count)
    half, wide = jnp.bfloat16, jnp.float32
    dma = pltpu.SemaphoreType.DMA
    vmem = pl.BlockSpec(memory_space=pltpu.VMEM)
    hbm = pl.BlockSpec(memory_space=pl.ANY)
    return pl.pallas_call(
        functools.partial(sums_kernel, count, ring, window),
        out_shape=(
            jax.ShapeDtypeStruct((2 * snps, window), half),
            jax.ShapeDtypeStruct((2 * window, window), half),
            jax.ShapeDtypeStruct((16, window), wide),
        ),
        in_specs=[hbm, vmem, vmem, hbm],
        out_specs=(vmem, vmem, vmem),
        scratch_shapes=[
            pltpu.VMEM((samples, snps), half),
            pltpu.VMEM(sign_flips.shape, jnp.int32),
            pltpu.VMEM((samples, window), half),
            pltpu.VMEM((samples, window), half),
            pltpu.VMEM((early_rows, window), half),
            pltpu.VMEM((count, early_per, window), half),
            pltpu.VMEM((early_per, window), half),
            pltpu.VMEM((early_rows, window), half),
            pltpu.VMEM((window, window), half),
            pltpu.VMEM((count, late_per, window), half),
            pltpu.VMEM((late_per, window), half),
            pltpu.VMEM((window, window), half),
            pltpu.VMEM((2 * window, window), half),
            pltpu.VMEM((8, window), wide),
            pltpu.VMEM((8, window), wide),
            pltpu.VMEM((count, 8, window), wide),
            pltpu.VMEM((8, window), wide),
            dma((PARTS,)), dma((PARTS,)), dma((PARTS,)), dma((PARTS,)),
            dma((count,)), dma((count,)), dma((count,)), dma((count,)),
            dma((count,)), dma((count,)), dma((count,)), dma((count,)),
            dma((count,)), dma((count,)), dma((2,)), dma((2,)),
        ],
        compiler_params=pltpu.CompilerParams(collective_id=0, has_side_effects=True),
        name="sums",
    )(genotype, phenotype.reshape(-1, window), residual.reshape(-1, window), sign_flips)


def scores_kernel(
    sample_total, offset_ref, start_ref, end_ref, near, far, sums, member, weights, out, placed,
):
    genes, tissues, window = weights.shape
    padded = placed.shape[0] // genes
    blocks = near.shape[0] // window // 2
    per_block = genes // blocks
    offset = offset_ref[0]
    row, col = iotas(window, window)
    inverse = 1.0 / sample_total

    all_sums = jnp.concatenate([sums[...], jnp.zeros((window - 16, window), jnp.float32)], axis=0)
    by_column = all_sums.T
    lab_sum = all_sums[blocks:blocks + 1]

    def mean_row(b):
        at = b if b < blocks else 8
        return all_sums[at:at + 1] * inverse

    def mean_col(b):
        at = b if b < blocks else 8
        return by_column[:, at:at + 1] * inverse

    def block_at(b, band):
        if b == blocks:
            at, ref = (1 if band else 0), far
        elif band:
            at, ref = (1 + b if b < blocks - 1 else 2 * blocks - 1), near
        else:
            at, ref = (0 if b == 0 else blocks + b - 1), near
        return ref[pl.ds(at * window, window), :].astype(jnp.float32)

    def with_labels(b):
        centred = block_at(b, False) - mean_col(b) * lab_sum
        centred = pltpu.roll(centred, 1, 1)
        high = centred.astype(jnp.bfloat16)
        low = (centred - high.astype(jnp.float32)).astype(jnp.bfloat16)
        return jnp.concatenate([high, low], axis=1)

    def diagonal(b):
        value = block_at(b, True) * inverse - mean_col(b) * mean_row(b)
        return jnp.where(col > row, 2.0 * value, jnp.where(col == row, value, 0.0))

    def beside(b):
        value = block_at(b, True) * inverse - mean_col(b) * mean_row(b + 1)
        return jnp.where(col < row, 2.0 * value, 0.0)

    member_cols = member[...].astype(jnp.float32).T
    pos = lax.broadcasted_iota(jnp.int32, (1, window), 1)
    for g in range(genes):
        b = g // per_block
        start, end = start_ref[g], end_ref[g]
        inside = (pos < end - start).astype(jnp.float32)
        values = weights[g].astype(jnp.float32) * member_cols[:, g:g + 1] * inside
        values = jnp.concatenate([values, jnp.zeros_like(values)], axis=1)
        shift = start - offset - b * window
        placed[pl.ds(g * padded, tissues), :] = pltpu.roll(values, shift, 1)

    root = 1.0 / (sample_total ** 0.5)
    labelled = [with_labels(b) for b in range(blocks + 1)]
    for b in range(blocks):
        pair = jnp.concatenate([labelled[b], labelled[b + 1]], axis=0)
        band = jnp.concatenate([
            jnp.concatenate([diagonal(b), beside(b)], axis=1),
            jnp.concatenate([jnp.zeros((window, window), jnp.float32), diagonal(b + 1)], axis=1),
        ], axis=0).astype(jnp.bfloat16)
        for g in range(b * per_block, (b + 1) * per_block, 2):
            wide = placed[pl.ds(g * padded, 2 * padded), :]
            half = wide.astype(jnp.bfloat16)
            top = jnp.dot(half, pair, preferred_element_type=jnp.float32)
            square = jnp.dot(half, band, preferred_element_type=jnp.float32)
            variance = jnp.sum(square * wide, axis=1, keepdims=True)
            scale = lax.rsqrt(jnp.maximum(variance, 0.0) + 1e-06) * root
            scores = (top[:, :window] + top[:, window:]) * scale
            out[g] = scores[0:tissues]
            out[g + 1] = scores[padded:padded + tissues]


def on_device(genotype, phenotype, residual, sign_flips, weights, member, gene_start, gene_end):
    samples, snps = genotype.shape
    genes, tissues, window = weights.shape
    near, far, sums = reduced_sums(genotype, phenotype, residual, sign_flips, window)
    offset = (lax.axis_index("snp") * snps).astype(jnp.int32).reshape(1)
    padded = -(-tissues // 8) * 8
    vmem = pl.BlockSpec(memory_space=pltpu.VMEM)
    smem = pl.BlockSpec(memory_space=pltpu.SMEM)
    return pl.pallas_call(
        functools.partial(scores_kernel, samples * lax.axis_size("samp")),
        out_shape=jax.ShapeDtypeStruct(weights.shape, jnp.float32),
        in_specs=[smem, smem, smem, vmem, vmem, vmem, vmem, vmem],
        out_specs=vmem,
        scratch_shapes=[pltpu.VMEM((genes * padded, 2 * window), jnp.float32)],
        name="scores",
    )(offset, gene_start, gene_end, near, far, sums, member, weights)


def solution(mesh):
    return jax.shard_map(
        on_device,
        mesh=mesh,
        in_specs=(
            P("samp", "snp"),
            P("samp"),
            P("samp"),
            P("samp", None),
            P("snp", None, None),
            P("snp", None),
            P("snp"),
            P("snp"),
        ),
        out_specs=P("snp", None, None),
        check_vma=False,
    )
```

time: 114 us -> 31.9 us (0.28)
  the two profiles are of different devices: /device:TPU:0 before, /device:TPU:1 now
where the time goes in v1:
time: 31.9 us; the launch traced here: 31.7 us
  Pallas kernels  28.5 us (89%)
  local copies, waits for them, and re-layouts  3.15 us (10%)
    pallas_call x1, Pallas kernels, reduced_sums(): pl.pallas_call(functools.partial(sums_kernel, count, ring, window), out_s...  23.5 us
    pallas_call x1, Pallas kernels, on_device(): pl.pallas_call(functools.partial(scores_kernel, samples * lax.axis_size('...  5.01 us
    pallas_call x1, local copies, waits for them, and re-layouts, on_device(): pl.pallas_call(functools.partial(scores_kernel, samples * lax.axis_size('...  2.22 us
    unnamed x3, local copies, waits for them, and re-layouts  0.94 us

profile of v1, /device:TPU:1, one launch (start us, length us, event | category | flops | bytes accessed | tf_op | source)
XLA Modules:
  0.0 31.7 jit_solution(7913793048468846073)
XLA Ops:
  0.0 0.0 copy-start
  0.0 23.5 %sums.1 = (bf16[512,128]{1,0:T(8,128)(2,1)}, bf16[256,128]{1,0:T(8,128)(2,1)}, f32[16,128]{1,0:T(8,128)}) custom-call(bf16[2048,256]{1,0:T(8,128)(2,1)} %geno.1, f32[16,128]{1,0:T(8,128)} %bitcast.3, f32[16,128]{1,0:T(8,128)} %bitcast.4, s32[2048,127]{1,0:T(8,128)} %flips.1), custom_call_target="tpu_custom_call" | custom-call | tf_op jit(solution)/shard_map/sums/pallas_call | solution.py:259
  23.5 0.0 copy-done
  23.5 0.9 %copy.9.weights = bf16[32,49,128]{2,1,0:T(8,128)(2,1)} copy(bf16[32,49,128]{2,0,1:T(8,128)(2,1)S(1)} %copy-done) | data formatting | bytes 802816 | tf_op args[4]
  24.5 5.0 %scores.1 = f32[32,49,128]{2,1,0:T(8,128)} custom-call(s32[1]{0:T(128)} %bitcast.offset_ref, s32[32]{0:T(128)} %start_ref.1, s32[32]{0:T(128)} %end_ref.1, bf16[512,128]{1,0:T(8,128)(2,1)} %get-tuple-element.8.near, bf16[256,128]{1,0:T(8,128)(2,1)} %get-tuple-element.9.far, f32[16,128]{1,0:T(8,128)} %get-tuple-element.10.sums, s32[32,49]{1,0:T(8,128)} %member.1, ...), custom_call_target="tpu_custom_call" | custom-call | tf_op jit(solution)/shard_map/scores/pallas_call | solution.py:382
  29.5 2.2 %copy.10 = f32[32,49,128]{2,0,1:T(8,128)} copy(f32[32,49,128]{2,1,0:T(8,128)} %scores.1) | data formatting | bytes 1605632 | tf_op jit(solution)/shard_map/scores/pallas_call | solution.py:382
Async XLA Ops:
  0.0 23.5 %copy-start = (bf16[32,49,128]{2,0,1:T(8,128)(2,1)S(1)}, bf16[32,49,128]{2,0,1:T(8,128)(2,1)}, u32[]{:S(2)}) copy-start(bf16[32,49,128]{2,0,1:T(8,128)(2,1)} %param.12) | copy-start | bytes 1204228

commit v2 on v1

--- a/solution.py
+++ b/solution.py
@@ -40,14 +40,14 @@
 
 def sums_kernel(
     count, ring, window,
-    geno, phen, resid, flips,
-    near_out, far_out, sums_out,
+    geno, phen, resid, flips, starts, ends, member, weights,
+    near_out, far_out, sums_out, corner_out, placed_out,
     geno_v, flips_v, halo_v, labels_v,
     early_s, early_r, early_p, early_g,
-    late_s, late_r, late_p, late_g,
+    late_s, late_r,
     tail_v, tail_sums, sums_s, sums_r, sums_t,
     load_sem, flip_sem, halo_ss, halo_rs,
-    es_ss, es_rs, eg_ss, eg_rs, ls_ss, ls_rs, lg_ss, lg_rs,
+    es_ss, es_rs, eg_ss, eg_rs, lt_ss, lt_rs,
     sm_ss, sm_rs, tl_ss, tl_rs,
 ):
     me = lax.axis_index("samp")
@@ -87,6 +87,19 @@
         barrier, inc=1, device_id=(ahead(dist), mine), device_id_type=MESH))
     for other in (before, after):
         pl.semaphore_signal(barrier, inc=1, device_id=(me, other), device_id_type=MESH)
+
+    flip_count = flips_v.shape[1]
+    phen_cols = columns_of(phen)
+    resid_cols = columns_of(resid)
+    lanes = phen.shape[1]
+    for i in range(PARTS):
+        flip_loads[i].wait()
+        for t in range(i * part // lanes, (i + 1) * part // lanes):
+            rows = pl.ds(t * lanes, lanes)
+            signs = flips_v[rows, :].astype(jnp.float32)
+            labels_v[rows, pl.ds(0, flip_count)] = (signs * resid_cols[:, t:t + 1]).astype(jnp.bfloat16)
+            labels_v[rows, pl.ds(flip_count, 1)] = phen_cols[:, t:t + 1].astype(jnp.bfloat16)
+
     pl.semaphore_wait(barrier, count + 1)
 
     def remote(src, dst, ss, rs, device):
@@ -158,18 +171,6 @@
         guarded(owners, me, lambda: peers(
             lambda dist: gather_copy(piece, full, gss, grs, per, dist).wait_send()))
 
-    flip_count = flips_v.shape[1]
-    phen_cols = columns_of(phen)
-    resid_cols = columns_of(resid)
-    lanes = phen.shape[1]
-    for i in range(PARTS):
-        flip_loads[i].wait()
-        for t in range(i * part // lanes, (i + 1) * part // lanes):
-            rows = pl.ds(t * lanes, lanes)
-            signs = flips_v[rows, :].astype(jnp.float32)
-            labels_v[rows, pl.ds(0, flip_count)] = (signs * resid_cols[:, t:t + 1]).astype(jnp.bfloat16)
-            labels_v[rows, pl.ds(flip_count, 1)] = phen_cols[:, t:t + 1].astype(jnp.bfloat16)
-
     for i in range(PARTS):
         loads[i].wait()
     own = geno_v[...]
@@ -189,51 +190,63 @@
         return remote(sums_s, sums_r.at[dist], sm_ss.at[dist], sm_rs.at[dist], (ahead(dist), mine))
 
     row, col = iotas(window, window)
-    early_s[pl.ds(0, window), :] = with_labels[0:window].astype(jnp.bfloat16)
-    for b in range(blocks - 1):
+    for b in range(blocks):
         low, mid, high = b * window, (b + 1) * window, (b + 2) * window
-        band = jnp.where(col >= row, gram[low:mid, low:mid], gram[low:mid, mid:high])
-        early_s[pl.ds((1 + b) * window, window), :] = band.astype(jnp.bfloat16)
-        early_s[pl.ds((blocks + b) * window, window), :] = with_labels[mid:high].astype(jnp.bfloat16)
-    early_per, late_per = early_p.shape[0], late_p.shape[0]
+        beyond = gram[low:mid, mid:high] if b < blocks - 1 else 0.0
+        early_s[pl.ds(2 * low, window), :] = with_labels[low:mid].astype(jnp.bfloat16)
+        band = jnp.where(col >= row, gram[low:mid, low:mid], beyond)
+        early_s[pl.ds(2 * low + window, window), :] = band.astype(jnp.bfloat16)
+    early_per = early_p.shape[0]
     scatter_start(early_s, early_r, es_ss, es_rs, early_per)
     peers(lambda dist: sums_copy(dist).start())
 
+    place(mine * snps, starts, ends, member, weights, placed_out)
+    reduce_and_gather(early_s, early_r, early_p, early_g, es_ss, es_rs, eg_ss, eg_rs, early_per)
+
     last = snps - window
-    with_halo = jnp.zeros((window, window), jnp.float32)
+    corner = jnp.zeros((window, window), jnp.float32)
     for i in range(PARTS):
         rows = pl.ds(i * part, part)
         halos[i].wait_recv()
-        with_halo += across(geno_v[rows, pl.ds(last, window)], halo_v[rows, :])
-    late_s[...] = jnp.where(col >= row, gram[last:, last:], with_halo).astype(jnp.bfloat16)
-    scatter_start(late_s, late_r, ls_ss, ls_rs, late_per)
-
-    reduce_and_gather(early_s, early_r, early_p, early_g, es_ss, es_rs, eg_ss, eg_rs, early_per)
-
-    sums_total = sums_s[...]
-    if count <= 16:
-        for dist in range(1, count):
-            sums_copy(dist).wait_recv()
-            sums_total += sums_r[dist]
-    else:
+        corner += across(geno_v[rows, pl.ds(last, window)], halo_v[rows, :])
+    mid = window // 2
+    half_row, half_col = iotas(mid, window)
+    turned = pltpu.roll(corner, mid, 1)[:mid]
+    folded = jnp.where(half_col - mid > half_row, corner.T[mid:], turned)
+    late_s[...] = jnp.where(half_col < mid, corner[mid:], folded).astype(jnp.bfloat16)
+
+    def late_copy(dist):
+        return remote(late_s, late_r.at[dist], lt_ss.at[dist], lt_rs.at[dist], (ahead(dist), mine))
+
+    peers(lambda dist: late_copy(dist).start())
+
+    def collect(make, got, total):
+        if count <= 16:
+            for dist in range(1, count):
+                make(dist).wait_recv()
+                total += got[dist].astype(jnp.float32)
+            return total
+
         def step(dist, total):
-            sums_copy(dist).wait_recv()
-            return total + sums_r[dist]
-        sums_total = lax.fori_loop(1, count, step, sums_total)
-    sums_t[...] = sums_total
+            make(dist).wait_recv()
+            return total + got[dist].astype(jnp.float32)
+        return lax.fori_loop(1, count, step, total)
+
+    sums_t[...] = collect(sums_copy, sums_r, sums_s[...])
     tail_copies = [remote(sums_t, tail_sums, tl_ss.at[0], tl_rs.at[0], (me, before))]
     tail_copies[0].start()
-
-    reduce_and_gather(late_s, late_r, late_p, late_g, ls_ss, ls_rs, lg_ss, lg_rs, late_per)
-
     gather_wait(early_s, early_p, early_g, eg_ss, eg_rs, early_per)
     tail_copies.append(remote(
         early_g.at[pl.ds(0, 2 * window)], tail_v, tl_ss.at[1], tl_rs.at[1], (me, before)))
     tail_copies[1].start()
-    near_out[pl.ds(0, early_g.shape[0]), :] = early_g[...]
-    gather_wait(late_s, late_p, late_g, lg_ss, lg_rs, late_per)
-    near_out[pl.ds(early_g.shape[0], window), :] = late_g[...]
+    near_out[...] = early_g[...]
     sums_out[pl.ds(0, 8), :] = sums_t[...]
+
+    folded = collect(late_copy, late_r, late_s[...].astype(jnp.float32))
+    mirrored = jnp.concatenate([folded, folded], axis=0).T
+    corner_out[pl.ds(0, mid), :] = pltpu.roll(folded, mid, 1)
+    corner_out[pl.ds(mid, mid), :] = jnp.where(half_col < mid, folded, mirrored[mid:])
+
     for copy in tail_copies:
         copy.wait_recv()
     far_out[...] = tail_v[...]
@@ -242,16 +255,50 @@
     for copy in halos + tail_copies:
         copy.wait_send()
     sends_wait(early_s, early_r, early_p, early_g, es_ss, es_rs, eg_ss, eg_rs, early_per)
-    sends_wait(late_s, late_r, late_p, late_g, ls_ss, ls_rs, lg_ss, lg_rs, late_per)
     peers(lambda dist: sums_copy(dist).wait_send())
-
-
-def reduced_sums(genotype, phenotype, residual, sign_flips, window):
+    peers(lambda dist: late_copy(dist).wait_send())
+
+
+def place(offset, starts, ends, member, weights, placed):
+    tissues, genes, window = weights.shape
+    blocks = placed.shape[0]
+    per_block = genes // blocks
+    spacing = window // per_block
+    gene_row, gene_col = iotas(genes, genes)
+
+    def upright(row_ref):
+        spread = jnp.broadcast_to(row_ref[...].astype(jnp.float32), (genes, genes))
+        picked = jnp.where(gene_row == gene_col, spread, 0.0)
+        return jnp.sum(picked, axis=1, keepdims=True).astype(jnp.int32)
+
+    first, past = upright(starts), upright(ends)
+    gene, lane = iotas(genes, window)
+    inside = (lane < past - first).astype(jnp.float32)
+    within = first - offset - (gene // per_block) * window
+    extra = within - (gene % per_block) * spacing
+    owned = member[...].astype(jnp.float32)
+    for t in range(tissues):
+        values = weights[t].astype(jnp.float32) * owned[:, t:t + 1] * inside
+        bit = 1
+        while bit < spacing:
+            values = jnp.where((extra & bit) != 0, pltpu.roll(values, bit, 1), values)
+            bit *= 2
+        for b in range(blocks):
+            genes_of = slice(b * per_block, (b + 1) * per_block)
+            turned = pltpu.roll(values[genes_of], 0, 1, stride=spacing, stride_axis=0)
+            kept = lane[genes_of] >= within[genes_of]
+            rows = pl.ds(t * per_block, per_block)
+            placed[b, rows, pl.ds(0, window)] = jnp.where(kept, turned, 0.0).astype(jnp.bfloat16)
+            placed[b, rows, pl.ds(window, window)] = jnp.where(kept, 0.0, turned).astype(jnp.bfloat16)
+
+
+def reduced_sums(genotype, phenotype, residual, sign_flips, starts, ends, member, weights):
     samples, snps = genotype.shape
+    tissues, genes, window = weights.shape
     count, ring = lax.axis_size("samp"), lax.axis_size("snp")
     blocks = snps // window
-    early_rows = (2 * blocks - 1) * window
-    early_per, late_per = share_of(early_rows, count), share_of(window, count)
+    early_rows = 2 * snps
+    early_per = share_of(early_rows, count)
     half, wide = jnp.bfloat16, jnp.float32
     dma = pltpu.SemaphoreType.DMA
     vmem = pl.BlockSpec(memory_space=pltpu.VMEM)
@@ -259,12 +306,14 @@
     return pl.pallas_call(
         functools.partial(sums_kernel, count, ring, window),
         out_shape=(
-            jax.ShapeDtypeStruct((2 * snps, window), half),
+            jax.ShapeDtypeStruct((early_rows, window), half),
             jax.ShapeDtypeStruct((2 * window, window), half),
             jax.ShapeDtypeStruct((16, window), wide),
+            jax.ShapeDtypeStruct((window, window), wide),
+            jax.ShapeDtypeStruct((blocks, tissues * genes // blocks, 2 * window), half),
         ),
-        in_specs=[hbm, vmem, vmem, hbm],
-        out_specs=(vmem, vmem, vmem),
+        in_specs=[hbm, vmem, vmem, hbm, vmem, vmem, vmem, vmem],
+        out_specs=(vmem,) * 5,
         scratch_shapes=[
             pltpu.VMEM((samples, snps), half),
             pltpu.VMEM(sign_flips.shape, jnp.int32),
@@ -274,10 +323,8 @@
             pltpu.VMEM((count, early_per, window), half),
             pltpu.VMEM((early_per, window), half),
             pltpu.VMEM((early_rows, window), half),
-            pltpu.VMEM((window, window), half),
-            pltpu.VMEM((count, late_per, window), half),
-            pltpu.VMEM((late_per, window), half),
-            pltpu.VMEM((window, window), half),
+            pltpu.VMEM((window // 2, window), half),
+            pltpu.VMEM((count, window // 2, window), half),
             pltpu.VMEM((2 * window, window), half),
             pltpu.VMEM((8, window), wide),
             pltpu.VMEM((8, window), wide),
@@ -285,22 +332,21 @@
             pltpu.VMEM((8, window), wide),
             dma((PARTS,)), dma((PARTS,)), dma((PARTS,)), dma((PARTS,)),
             dma((count,)), dma((count,)), dma((count,)), dma((count,)),
-            dma((count,)), dma((count,)), dma((count,)), dma((count,)),
+            dma((count,)), dma((count,)),
             dma((count,)), dma((count,)), dma((2,)), dma((2,)),
         ],
         compiler_params=pltpu.CompilerParams(collective_id=0, has_side_effects=True),
         name="sums",
-    )(genotype, phenotype.reshape(-1, window), residual.reshape(-1, window), sign_flips)
-
-
-def scores_kernel(
-    sample_total, offset_ref, start_ref, end_ref, near, far, sums, member, weights, out, placed,
-):
-    genes, tissues, window = weights.shape
-    padded = placed.shape[0] // genes
-    blocks = near.shape[0] // window // 2
+    )(
+        genotype, phenotype.reshape(-1, window), residual.reshape(-1, window), sign_flips,
+        starts.reshape(1, genes), ends.reshape(1, genes), member, weights,
+    )
+
+
+def scores_kernel(sample_total, near, far, sums, corner, placed, out_hbm, out, sem):
+    tissues, genes, window = out.shape
+    blocks, rows_in_block, _ = placed.shape
     per_block = genes // blocks
-    offset = offset_ref[0]
     row, col = iotas(window, window)
     inverse = 1.0 / sample_total
 
@@ -317,76 +363,70 @@
         return by_column[:, at:at + 1] * inverse
 
     def block_at(b, band):
-        if b == blocks:
-            at, ref = (1 if band else 0), far
-        elif band:
-            at, ref = (1 + b if b < blocks - 1 else 2 * blocks - 1), near
-        else:
-            at, ref = (0 if b == 0 else blocks + b - 1), near
+        ref, at = (near, 2 * b + band) if b < blocks else (far, band)
         return ref[pl.ds(at * window, window), :].astype(jnp.float32)
 
     def with_labels(b):
-        centred = block_at(b, False) - mean_col(b) * lab_sum
+        centred = block_at(b, 0) - mean_col(b) * lab_sum
         centred = pltpu.roll(centred, 1, 1)
         high = centred.astype(jnp.bfloat16)
         low = (centred - high.astype(jnp.float32)).astype(jnp.bfloat16)
         return jnp.concatenate([high, low], axis=1)
 
     def diagonal(b):
-        value = block_at(b, True) * inverse - mean_col(b) * mean_row(b)
+        value = block_at(b, 1) * inverse - mean_col(b) * mean_row(b)
         return jnp.where(col > row, 2.0 * value, jnp.where(col == row, value, 0.0))
 
     def beside(b):
-        value = block_at(b, True) * inverse - mean_col(b) * mean_row(b + 1)
+        products = block_at(b, 1) if b < blocks - 1 else corner[...]
+        value = products * inverse - mean_col(b) * mean_row(b + 1)
         return jnp.where(col < row, 2.0 * value, 0.0)
-
-    member_cols = member[...].astype(jnp.float32).T
-    pos = lax.broadcasted_iota(jnp.int32, (1, window), 1)
-    for g in range(genes):
-        b = g // per_block
-        start, end = start_ref[g], end_ref[g]
-        inside = (pos < end - start).astype(jnp.float32)
-        values = weights[g].astype(jnp.float32) * member_cols[:, g:g + 1] * inside
-        values = jnp.concatenate([values, jnp.zeros_like(values)], axis=1)
-        shift = start - offset - b * window
-        placed[pl.ds(g * padded, tissues), :] = pltpu.roll(values, shift, 1)
 
     root = 1.0 / (sample_total ** 0.5)
     labelled = [with_labels(b) for b in range(blocks + 1)]
+    pairs, bands = [], []
     for b in range(blocks):
-        pair = jnp.concatenate([labelled[b], labelled[b + 1]], axis=0)
-        band = jnp.concatenate([
+        pairs.append(jnp.concatenate([labelled[b], labelled[b + 1]], axis=0))
+        bands.append(jnp.concatenate([
             jnp.concatenate([diagonal(b), beside(b)], axis=1),
             jnp.concatenate([jnp.zeros((window, window), jnp.float32), diagonal(b + 1)], axis=1),
-        ], axis=0).astype(jnp.bfloat16)
-        for g in range(b * per_block, (b + 1) * per_block, 2):
-            wide = placed[pl.ds(g * padded, 2 * padded), :]
-            half = wide.astype(jnp.bfloat16)
-            top = jnp.dot(half, pair, preferred_element_type=jnp.float32)
-            square = jnp.dot(half, band, preferred_element_type=jnp.float32)
-            variance = jnp.sum(square * wide, axis=1, keepdims=True)
+        ], axis=0).astype(jnp.bfloat16))
+
+    copies = []
+    step = next(n for n in range(min(7, tissues), 0, -1) if tissues % n == 0)
+    for t in range(0, tissues, step):
+        for b in range(blocks):
+            half = placed[b, pl.ds(t * per_block, step * per_block), :]
+            top = jnp.dot(half, pairs[b], preferred_element_type=jnp.float32)
+            square = jnp.dot(half, bands[b], preferred_element_type=jnp.float32)
+            variance = jnp.sum(square * half.astype(jnp.float32), axis=1, keepdims=True)
             scale = lax.rsqrt(jnp.maximum(variance, 0.0) + 1e-06) * root
             scores = (top[:, :window] + top[:, window:]) * scale
-            out[g] = scores[0:tissues]
-            out[g + 1] = scores[padded:padded + tissues]
+            out[pl.ds(t, step), pl.ds(b * per_block, per_block), :] = scores.reshape(step, per_block, window)
+        part = pl.ds(t, step)
+        copies.append(pltpu.make_async_copy(out.at[part], out_hbm.at[part], sem.at[t // step]))
+        copies[-1].start()
+    for copy in copies:
+        copy.wait()
 
 
 def on_device(genotype, phenotype, residual, sign_flips, weights, member, gene_start, gene_end):
-    samples, snps = genotype.shape
-    genes, tissues, window = weights.shape
-    near, far, sums = reduced_sums(genotype, phenotype, residual, sign_flips, window)
-    offset = (lax.axis_index("snp") * snps).astype(jnp.int32).reshape(1)
-    padded = -(-tissues // 8) * 8
+    by_tissue = weights.transpose(1, 0, 2)
+    near, far, sums, corner, placed = reduced_sums(
+        genotype, phenotype, residual, sign_flips, gene_start, gene_end, member, by_tissue)
     vmem = pl.BlockSpec(memory_space=pltpu.VMEM)
-    smem = pl.BlockSpec(memory_space=pltpu.SMEM)
-    return pl.pallas_call(
-        functools.partial(scores_kernel, samples * lax.axis_size("samp")),
-        out_shape=jax.ShapeDtypeStruct(weights.shape, jnp.float32),
-        in_specs=[smem, smem, smem, vmem, vmem, vmem, vmem, vmem],
-        out_specs=vmem,
-        scratch_shapes=[pltpu.VMEM((genes * padded, 2 * window), jnp.float32)],
+    scores = pl.pallas_call(
+        functools.partial(scores_kernel, genotype.shape[0] * lax.axis_size("samp")),
+        out_shape=jax.ShapeDtypeStruct(by_tissue.shape, jnp.float32),
+        in_specs=[vmem] * 5,
+        out_specs=pl.BlockSpec(memory_space=pl.ANY),
+        scratch_shapes=[
+            pltpu.VMEM(by_tissue.shape, jnp.float32),
+            pltpu.SemaphoreType.DMA((by_tissue.shape[0],)),
+        ],
         name="scores",
-    )(offset, gene_start, gene_end, near, far, sums, member, weights)
+    )(near, far, sums, corner, placed)
+    return scores.transpose(1, 0, 2)
 
 
 def solution(mesh):

time: 31.9 us -> 26.2 us (0.82)
  local copies, waits for them, and re-layouts: 3.15 us -> 0 us
  Pallas kernels: 28.5 us -> 26 us
    pallas_call x1 -> x0, local copies, waits for them, and re-layouts: 2.22 us -> none  [on_device(): pl.pallas_call(functools.partial(scores_kernel, samples * lax.axis_size('...]
    pallas_call x1, Pallas kernels: 5.01 us -> 3.31 us  [on_device(): pl.pallas_call(functools.partial(scores_kernel, genotype.shape[0] * lax.a...]
    unnamed x3 -> x0, local copies, waits for them, and re-layouts: 0.94 us -> none
    pallas_call x1, Pallas kernels: 23.5 us -> 22.7 us  [reduced_sums(): pl.pallas_call(functools.partial(sums_kernel, count, ring, window), out_s...]
where the time goes in v2:
time: 26.2 us; the launch traced here: 26 us
  Pallas kernels  26 us (99%)
    pallas_call x1, Pallas kernels, reduced_sums(): pl.pallas_call(functools.partial(sums_kernel, count, ring, window), out_s...  22.7 us
    pallas_call x1, Pallas kernels, on_device(): pl.pallas_call(functools.partial(scores_kernel, genotype.shape[0] * lax.a...  3.31 us

profile of v2, /device:TPU:1, one launch (start us, length us, event | category | flops | bytes accessed | tf_op | source)
XLA Modules:
  0.0 26.0 jit_solution(12141754947327262124)
XLA Ops:
  0.0 22.7 %sums.1 = (bf16[512,128]{1,0:T(8,128)(2,1)}, bf16[256,128]{1,0:T(8,128)(2,1)}, f32[16,128]{1,0:T(8,128)}, f32[128,128]{1,0:T(8,128)}, bf16[2,784,256]{2,1,0:T(8,128)(2,1)}) custom-call(bf16[2048,256]{1,0:T(8,128)(2,1)} %geno.1, f32[16,128]{1,0:T(8,128)} %bitcast.7, f32[16,128]{1,0:T(8,128)} %bitcast.8, s32[2048,127]{1,0:T(8,128)} %flips.1, s32[1,32]{1,0:T(1,128)} %bitcast.9, ...), custom_call_target="tpu_custom_call" | custom-call | tf_op jit(solution)/shard_map/sums/pallas_call | solution.py:306
  22.7 3.3 %scores.1 = f32[49,32,128]{2,1,0:T(8,128)} custom-call(bf16[512,128]{1,0:T(8,128)(2,1)} %get-tuple-element.10.near, bf16[256,128]{1,0:T(8,128)(2,1)} %get-tuple-element.11.far, f32[16,128]{1,0:T(8,128)} %get-tuple-element.12.sums, f32[128,128]{1,0:T(8,128)} %get-tuple-element.13.corner, bf16[2,784,256]{2,1,0:T(8,128)(2,1)} %get-tuple-element.14.placed), custom_call_target="tpu_custom_call" | custom-call | tf_op jit(solution)/shard_map/scores/pallas_call | solution.py:418

commit v3 on v2

--- a/solution.py
+++ b/solution.py
@@ -41,14 +41,14 @@
 def sums_kernel(
     count, ring, window,
     geno, phen, resid, flips, starts, ends, member, weights,
-    near_out, far_out, sums_out, corner_out, placed_out,
+    near_out, far_out, sums_out, corner_out, placed_hbm,
     geno_v, flips_v, halo_v, labels_v,
     early_s, early_r, early_p, early_g,
     late_s, late_r,
-    tail_v, tail_sums, sums_s, sums_r, sums_t,
-    load_sem, flip_sem, halo_ss, halo_rs,
+    weights_v, placed_v, tail_v, tail_sums, sums_s, sums_r, sums_t,
+    load_sem, flip_sem, side_sem, halo_ss, halo_rs,
     es_ss, es_rs, eg_ss, eg_rs, lt_ss, lt_rs,
-    sm_ss, sm_rs, tl_ss, tl_rs,
+    sm_ss, sm_rs, tl_ss, tl_rs, fg_ss, fg_rs,
 ):
     me = lax.axis_index("samp")
     mine = lax.axis_index("snp")
@@ -65,6 +65,10 @@
         flip_loads.append(pltpu.make_async_copy(flips.at[rows], flips_v.at[rows], flip_sem.at[i]))
         loads[i].start()
         flip_loads[i].start()
+
+    weights_load = pltpu.make_async_copy(weights, weights_v, side_sem.at[0])
+    weights_load.start()
+    placed_save = pltpu.make_async_copy(placed_v, placed_hbm, side_sem.at[1])
 
     def peers(body):
         if count <= 16:
@@ -76,6 +80,10 @@
                 return carry
             lax.fori_loop(1, count, step, 0)
 
+    def everyone(body):
+        body(0)
+        peers(body)
+
     def ahead(dist):
         return lax.rem(me + dist, count)
 
@@ -86,7 +94,8 @@
     peers(lambda dist: pl.semaphore_signal(
         barrier, inc=1, device_id=(ahead(dist), mine), device_id_type=MESH))
     for other in (before, after):
-        pl.semaphore_signal(barrier, inc=1, device_id=(me, other), device_id_type=MESH)
+        everyone(lambda dist: pl.semaphore_signal(
+            barrier, inc=1, device_id=(ahead(dist), other), device_id_type=MESH))
 
     flip_count = flips_v.shape[1]
     phen_cols = columns_of(phen)
@@ -100,7 +109,7 @@
             labels_v[rows, pl.ds(0, flip_count)] = (signs * resid_cols[:, t:t + 1]).astype(jnp.bfloat16)
             labels_v[rows, pl.ds(flip_count, 1)] = phen_cols[:, t:t + 1].astype(jnp.bfloat16)
 
-    pl.semaphore_wait(barrier, count + 1)
+    pl.semaphore_wait(barrier, 3 * count - 1)
 
     def remote(src, dst, ss, rs, device):
         return pltpu.make_async_remote_copy(
@@ -128,6 +137,21 @@
     def gather_copy(piece, full, ss, rs, per, dist):
         start = pl.multiple_of(me * per, TILE)
         return remote(piece, full.at[pl.ds(start, per)], ss.at[dist], rs.at[dist], (ahead(dist), mine))
+
+    far_owners = tail_v.shape[0] // early_p.shape[0]
+
+    def far_copy(dist):
+        per = early_p.shape[0]
+        start = pl.multiple_of(me * per, TILE)
+        return remote(
+            early_p, tail_v.at[pl.ds(start, per)], fg_ss.at[dist], fg_rs.at[dist], (ahead(dist), before))
+
+    def far_wait(dist):
+        per = early_p.shape[0]
+        start = pl.multiple_of(behind(dist) * per, TILE)
+        guarded(far_owners, behind(dist), lambda: remote(
+            early_p, tail_v.at[pl.ds(start, per)], fg_ss.at[dist], fg_rs.at[dist],
+            (ahead(dist), before)).wait_recv())
 
     def scatter_start(buf, got, ss, rs, per):
         owners = buf.shape[0] // per
@@ -152,6 +176,7 @@
                 total = lax.fori_loop(1, count, step, total)
             piece[...] = total.astype(piece.dtype)
             peers(lambda dist: gather_copy(piece, full, gss, grs, per, dist).start())
+            guarded(far_owners, me, lambda: everyone(lambda dist: far_copy(dist).start()))
             full[rows, :] = piece[...]
         guarded(owners, me, owner)
 
@@ -200,7 +225,9 @@
     scatter_start(early_s, early_r, es_ss, es_rs, early_per)
     peers(lambda dist: sums_copy(dist).start())
 
-    place(mine * snps, starts, ends, member, weights, placed_out)
+    weights_load.wait()
+    place(mine * snps, starts, ends, member, weights_v, placed_v)
+    placed_save.start()
     reduce_and_gather(early_s, early_r, early_p, early_g, es_ss, es_rs, eg_ss, eg_rs, early_per)
 
     last = snps - window
@@ -236,9 +263,6 @@
     tail_copies = [remote(sums_t, tail_sums, tl_ss.at[0], tl_rs.at[0], (me, before))]
     tail_copies[0].start()
     gather_wait(early_s, early_p, early_g, eg_ss, eg_rs, early_per)
-    tail_copies.append(remote(
-        early_g.at[pl.ds(0, 2 * window)], tail_v, tl_ss.at[1], tl_rs.at[1], (me, before)))
-    tail_copies[1].start()
     near_out[...] = early_g[...]
     sums_out[pl.ds(0, 8), :] = sums_t[...]
 
@@ -249,6 +273,7 @@
 
     for copy in tail_copies:
         copy.wait_recv()
+    everyone(far_wait)
     far_out[...] = tail_v[...]
     sums_out[pl.ds(8, 8), :] = tail_sums[...]
 
@@ -257,6 +282,8 @@
     sends_wait(early_s, early_r, early_p, early_g, es_ss, es_rs, eg_ss, eg_rs, early_per)
     peers(lambda dist: sums_copy(dist).wait_send())
     peers(lambda dist: late_copy(dist).wait_send())
+    guarded(far_owners, me, lambda: everyone(lambda dist: far_copy(dist).wait_send()))
+    placed_save.wait()
 
 
 def place(offset, starts, ends, member, weights, placed):
@@ -312,8 +339,8 @@
             jax.ShapeDtypeStruct((window, window), wide),
             jax.ShapeDtypeStruct((blocks, tissues * genes // blocks, 2 * window), half),
         ),
-        in_specs=[hbm, vmem, vmem, hbm, vmem, vmem, vmem, vmem],
-        out_specs=(vmem,) * 5,
+        in_specs=[hbm, vmem, vmem, hbm, vmem, vmem, vmem, hbm],
+        out_specs=(vmem,) * 4 + (hbm,),
         scratch_shapes=[
             pltpu.VMEM((samples, snps), half),
             pltpu.VMEM(sign_flips.shape, jnp.int32),
@@ -325,15 +352,18 @@
             pltpu.VMEM((early_rows, window), half),
             pltpu.VMEM((window // 2, window), half),
             pltpu.VMEM((count, window // 2, window), half),
+            pltpu.VMEM(weights.shape, half),
+            pltpu.VMEM((blocks, tissues * genes // blocks, 2 * window), half),
             pltpu.VMEM((2 * window, window), half),
             pltpu.VMEM((8, window), wide),
             pltpu.VMEM((8, window), wide),
             pltpu.VMEM((count, 8, window), wide),
             pltpu.VMEM((8, window), wide),
-            dma((PARTS,)), dma((PARTS,)), dma((PARTS,)), dma((PARTS,)),
+            dma((PARTS,)), dma((PARTS,)), dma((2,)), dma((PARTS,)), dma((PARTS,)),
             dma((count,)), dma((count,)), dma((count,)), dma((count,)),
             dma((count,)), dma((count,)),
-            dma((count,)), dma((count,)), dma((2,)), dma((2,)),
+            dma((count,)), dma((count,)), dma((1,)), dma((1,)),
+            dma((count,)), dma((count,)),
         ],
         compiler_params=pltpu.CompilerParams(collective_id=0, has_side_effects=True),
         name="sums",

time: 26.2 us -> 30.1 us (1.15)
  the two profiles are of different devices: /device:TPU:1 before, /device:TPU:27 now
where the time goes in v3:
time: 30.1 us; the launch traced here: 29.8 us
  Pallas kernels  29.8 us (99%)
    pallas_call x1, Pallas kernels, reduced_sums(): pl.pallas_call(functools.partial(sums_kernel, count, ring, window), out_s...  26.5 us
    pallas_call x1, Pallas kernels, on_device(): pl.pallas_call(functools.partial(scores_kernel, genotype.shape[0] * lax.a...  3.31 us

profile of v3, /device:TPU:27, one launch (start us, length us, event | category | flops | bytes accessed | tf_op | source)
XLA Modules:
  0.0 29.8 jit_solution(16552864136477304434)
XLA Ops:
  0.0 26.5 %sums.1 = (bf16[512,128]{1,0:T(8,128)(2,1)}, bf16[256,128]{1,0:T(8,128)(2,1)}, f32[16,128]{1,0:T(8,128)}, f32[128,128]{1,0:T(8,128)}, bf16[2,784,256]{2,1,0:T(8,128)(2,1)}) custom-call(bf16[2048,256]{1,0:T(8,128)(2,1)} %geno.1, f32[16,128]{1,0:T(8,128)} %bitcast.7, f32[16,128]{1,0:T(8,128)} %bitcast.8, s32[2048,127]{1,0:T(8,128)} %flips.1, s32[1,32]{1,0:T(1,128)} %bitcast.9, ...), custom_call_target="tpu_custom_call" | custom-call | tf_op jit(solution)/shard_map/sums/pallas_call | solution.py:333
  26.5 3.3 %scores.1 = f32[49,32,128]{2,1,0:T(8,128)} custom-call(bf16[512,128]{1,0:T(8,128)(2,1)} %get-tuple-element.10.near, bf16[256,128]{1,0:T(8,128)(2,1)} %get-tuple-element.11.far, f32[16,128]{1,0:T(8,128)} %get-tuple-element.12.sums, f32[128,128]{1,0:T(8,128)} %get-tuple-element.13.corner, bf16[2,784,256]{2,1,0:T(8,128)(2,1)} %get-tuple-element.14.placed), custom_call_target="tpu_custom_call" | custom-call | tf_op jit(solution)/shard_map/scores/pallas_call | solution.py:448

commit v4 on v2

--- a/solution.py
+++ b/solution.py
@@ -155,13 +155,15 @@
             full[rows, :] = piece[...]
         guarded(owners, me, owner)
 
-    def gather_wait(buf, piece, full, gss, grs, per):
-        owners = buf.shape[0] // per
-
+    def gather_wait(piece, full, gss, grs, per, low, high):
         def one(dist):
             start = pl.multiple_of(behind(dist) * per, TILE)
-            guarded(owners, behind(dist), lambda: remote(
-                piece, full.at[pl.ds(start, per)], gss.at[dist], grs.at[dist], (ahead(dist), mine)).wait_recv())
+
+            @pl.when((behind(dist) >= low) & (behind(dist) < high))
+            def _():
+                remote(
+                    piece, full.at[pl.ds(start, per)], gss.at[dist], grs.at[dist],
+                    (ahead(dist), mine)).wait_recv()
         peers(one)
 
     def sends_wait(buf, got, piece, full, ss, rs, gss, grs, per):
@@ -235,10 +237,12 @@
     sums_t[...] = collect(sums_copy, sums_r, sums_s[...])
     tail_copies = [remote(sums_t, tail_sums, tl_ss.at[0], tl_rs.at[0], (me, before))]
     tail_copies[0].start()
-    gather_wait(early_s, early_p, early_g, eg_ss, eg_rs, early_per)
+    first_owners = 2 * window // early_per
+    gather_wait(early_p, early_g, eg_ss, eg_rs, early_per, 0, first_owners)
     tail_copies.append(remote(
         early_g.at[pl.ds(0, 2 * window)], tail_v, tl_ss.at[1], tl_rs.at[1], (me, before)))
     tail_copies[1].start()
+    gather_wait(early_p, early_g, eg_ss, eg_rs, early_per, first_owners, early_s.shape[0] // early_per)
     near_out[...] = early_g[...]
     sums_out[pl.ds(0, 8), :] = sums_t[...]
 

time: 26.2 us -> 24.2 us (0.924)
  Pallas kernels: 26 us -> 24 us
    pallas_call x1, Pallas kernels: 22.7 us -> 20.7 us  [reduced_sums(): pl.pallas_call(functools.partial(sums_kernel, count, ring, window), out_s...]
where the time goes in v4:
time: 24.2 us; the launch traced here: 24 us
  Pallas kernels  24 us (99%)
    pallas_call x1, Pallas kernels, reduced_sums(): pl.pallas_call(functools.partial(sums_kernel, count, ring, window), out_s...  20.7 us
    pallas_call x1, Pallas kernels, on_device(): pl.pallas_call(functools.partial(scores_kernel, genotype.shape[0] * lax.a...  3.31 us

profile of v4, /device:TPU:1, one launch (start us, length us, event | category | flops | bytes accessed | tf_op | source)
XLA Modules:
  0.0 24.0 jit_solution(14201085055868957118)
XLA Ops:
  0.0 20.7 %sums.1 = (bf16[512,128]{1,0:T(8,128)(2,1)}, bf16[256,128]{1,0:T(8,128)(2,1)}, f32[16,128]{1,0:T(8,128)}, f32[128,128]{1,0:T(8,128)}, bf16[2,784,256]{2,1,0:T(8,128)(2,1)}) custom-call(bf16[2048,256]{1,0:T(8,128)(2,1)} %geno.1, f32[16,128]{1,0:T(8,128)} %bitcast.7, f32[16,128]{1,0:T(8,128)} %bitcast.8, s32[2048,127]{1,0:T(8,128)} %flips.1, s32[1,32]{1,0:T(1,128)} %bitcast.9, ...), custom_call_target="tpu_custom_call" | custom-call | tf_op jit(solution)/shard_map/sums/pallas_call | solution.py:310
  20.7 3.3 %scores.1 = f32[49,32,128]{2,1,0:T(8,128)} custom-call(bf16[512,128]{1,0:T(8,128)(2,1)} %get-tuple-element.10.near, bf16[256,128]{1,0:T(8,128)(2,1)} %get-tuple-element.11.far, f32[16,128]{1,0:T(8,128)} %get-tuple-element.12.sums, f32[128,128]{1,0:T(8,128)} %get-tuple-element.13.corner, bf16[2,784,256]{2,1,0:T(8,128)(2,1)} %get-tuple-element.14.placed), custom_call_target="tpu_custom_call" | custom-call | tf_op jit(solution)/shard_map/scores/pallas_call | solution.py:422
